TPU v7x, 32 devices: a whole 2x2x4 slice. The times are simulated.
32 devices in a mesh: grp: 4 (over x, core), seq: 8 (over z, y).
Axes of the slice: x: 2, y: 2, z: 4, core: 2. Of those that a mesh axis runs over, the one named last changes fastest.
Arguments:
- signal: float32 [64, 2048, 768], P('grp', 'seq'), may hold values from -36 to 36
- entry_gain: float32 [768], replicated
- entry_shift: float32 [768], replicated, may hold values from -3 to 3
- dilated_kernel: float32 [3, 768, 384], replicated
- middle_gain: float32 [384], replicated
- middle_shift: float32 [384], replicated, may hold values from -3 to 3
- pointwise_kernel: float32 [384, 768], replicated
- pointwise_bias: float32 [768], replicated, may hold values from -3 to 3
- lengths: int32 [64], replicated, may hold values from 128 to 1024, as said below
- assignment: int32 [4, 16], P('grp'), may hold values from 0 to 15, as said below
- cotangent: float32 [65536, 768], P(('grp', 'seq')), may hold values from -6 to 6
Outputs:
- activations: float32 [65536, 768], P(('grp', 'seq'))
- signal_gradient: float32 [64, 2048, 768], P('grp', 'seq')
- entry_gain_gradient: float32 [768], replicated
- entry_shift_gradient: float32 [768], replicated
- dilated_kernel_gradient: float32 [3, 768, 384], replicated
- middle_gain_gradient: float32 [384], replicated
- middle_shift_gradient: float32 [384], replicated
- pointwise_kernel_gradient: float32 [384, 768], replicated
- pointwise_bias_gradient: float32 [768], replicated
Inputs may be any that keep to these rules, and one draw needn't show every extreme that they name: `lengths`: valid rows of a window come first; some window is full with 1024 rows and some has exactly 128. `assignment`: each row lists the 16 windows of one group once.
All inputs are finite; a program needn't handle non-finite values.
Results may differ from a plain program's by a relative error of at most 0.0066.
Values may be sent and summed in bfloat16 or wider, within the bound.
No kernel may reach another device: no remote copies, remote signals or barrier semaphores. Data moves between devices by JAX's collectives and lax.ppermute only.
A program may use at most 128 MiB of HBM per device.

v0:
```python
import jax
import jax.numpy as jnp
from jax import lax
from jax.sharding import PartitionSpec as P

DILATION_STEP = 38
WINDOW_SPAN = 1024
HALF_WINDOW_ROWS = 512
EPSILON = 0.001


def from_partner(block, axis, bit):
    count = lax.axis_size(axis)
    route = []
    for low in range(count):
        high = low | 1 << bit
        if high != low and high < count:
            route += [(low, high), (high, low)]
    return lax.ppermute(block, axis, route)


def smooth(values):
    return jax.nn.gelu(values, approximate=True)


def moments(values, valid_mask, row_count):
    centre = lax.psum(jnp.sum(values * valid_mask, axis=(0, 1)), ("grp", "seq")) / row_count
    deviation = (values - centre) * valid_mask
    spread = lax.psum(jnp.sum(deviation * deviation, axis=(0, 1)), ("grp", "seq")) / row_count
    return (centre, lax.rsqrt(spread + EPSILON))


def extended(resident_rows, neighbour_border):
    position_count = resident_rows.shape[0]
    channel_width = resident_rows.shape[2]
    empty_row_block = jnp.zeros((position_count, DILATION_STEP, channel_width), resident_rows.dtype)
    bottom_portion = jnp.concatenate(
        [empty_row_block, resident_rows[:, :HALF_WINDOW_ROWS], neighbour_border[:, DILATION_STEP:]],
        axis=1,
    )
    top_portion = jnp.concatenate(
        [neighbour_border[:, :DILATION_STEP], resident_rows[:, HALF_WINDOW_ROWS:], empty_row_block],
        axis=1,
    )
    return jnp.stack([bottom_portion, top_portion], axis=1).reshape(
        2 * position_count, HALF_WINDOW_ROWS + 2 * DILATION_STEP, channel_width
    )


def per_device(
    signal,
    entry_gain,
    entry_shift,
    dilated_kernel,
    middle_gain,
    middle_shift,
    pointwise_kernel,
    pointwise_bias,
    lengths,
    assignment,
    cotangent,
):
    seq_count = lax.axis_size("seq")
    seq_place = lax.axis_index("seq")
    grp_place = lax.axis_index("grp")
    group_windows, segment, channel_width = signal.shape
    source_rows = segment // 2
    position_count = group_windows // seq_count
    bin_pairs = signal.reshape(group_windows, source_rows, 2, channel_width)
    first_bin = bin_pairs[:, :, 0]
    second_bin = bin_pairs[:, :, 1]
    take_first = first_bin >= second_bin
    group_lengths = lax.dynamic_slice_in_dim(lengths, grp_place * group_windows, group_windows)
    source_position = seq_place * source_rows + jnp.arange(source_rows, dtype=jnp.int32)
    source_valid = (source_position[None, :] < group_lengths[:, None]).astype(jnp.float32)[
        :, :, None
    ]
    pooled_low = (jnp.where(take_first, first_bin, second_bin) * source_valid).astype(jnp.bfloat16)
    window_order = assignment[0]
    upper_source = (seq_place >= seq_count // 2).astype(jnp.int32)
    targets = jnp.arange(seq_count, dtype=jnp.int32)
    slot_range = jnp.arange(position_count, dtype=jnp.int32)
    picked = window_order[
        (
            jnp.bitwise_xor(targets, upper_source)[:, None] * position_count + slot_range[None, :]
        ).reshape(-1)
    ]
    outgoing = jnp.take(pooled_low, picked, axis=0)
    arrived = lax.all_to_all(outgoing, "seq", split_axis=0, concat_axis=1, tiled=True)
    partner_place = jnp.bitwise_xor(seq_place, 1)
    own_windows = lax.dynamic_slice_in_dim(window_order, seq_place * position_count, position_count)
    partner_windows = lax.dynamic_slice_in_dim(
        window_order, partner_place * position_count, position_count
    )
    row_position = jnp.arange(WINDOW_SPAN, dtype=jnp.int32)
    limit_rows = jnp.where(
        row_position[None, :] < HALF_WINDOW_ROWS,
        jnp.take(group_lengths, own_windows)[:, None],
        jnp.take(group_lengths, partner_windows)[:, None],
    )
    valid_mask = (row_position[None, :] < limit_rows).astype(jnp.float32)[:, :, None]
    row_count = jnp.sum(lengths.astype(jnp.float32))
    pooled = arrived.astype(jnp.float32)
    entry_centre, entry_scale = moments(pooled, valid_mask, row_count)
    entry_norm = (pooled - entry_centre) * entry_scale
    entry_smooth, entry_back = jax.vjp(smooth, entry_norm * entry_gain + entry_shift)
    entry_activation = (entry_smooth * valid_mask).astype(jnp.bfloat16)
    kernel_low = dilated_kernel.astype(jnp.bfloat16)
    entry_border = from_partner(
        entry_activation[:, HALF_WINDOW_ROWS - DILATION_STEP : HALF_WINDOW_ROWS + DILATION_STEP],
        "seq",
        0,
    )
    entry_widened = extended(entry_activation, entry_border)
    dilated_out = jnp.zeros(
        (2 * position_count, HALF_WINDOW_ROWS, kernel_low.shape[2]), jnp.float32
    )
    for kernel_tap_index in range(3):
        displaced_rows = entry_widened[
            :,
            kernel_tap_index * DILATION_STEP : kernel_tap_index * DILATION_STEP + HALF_WINDOW_ROWS,
        ]
        dilated_out = dilated_out + jnp.einsum(
            "hrc,cf->hrf",
            displaced_rows,
            kernel_low[kernel_tap_index],
            preferred_element_type=jnp.float32,
        )
    dilated_out = dilated_out.reshape(position_count, WINDOW_SPAN, -1)
    middle_centre, middle_scale = moments(dilated_out, valid_mask, row_count)
    middle_norm = (dilated_out - middle_centre) * middle_scale
    middle_smooth, middle_back = jax.vjp(smooth, middle_norm * middle_gain + middle_shift)
    middle_act = (middle_smooth * valid_mask).astype(jnp.bfloat16)
    pointwise_low = pointwise_kernel.astype(jnp.bfloat16)
    mixed_out = jnp.einsum(
        "krf,fd->krd", middle_act, pointwise_low, preferred_element_type=jnp.float32
    )
    activations = (valid_mask * (pooled + mixed_out + pointwise_bias)).reshape(-1, channel_width)
    grad_block = cotangent.reshape(position_count, WINDOW_SPAN, channel_width) * valid_mask
    grad_mixed = grad_block.astype(jnp.bfloat16)
    bias_part = jnp.sum(grad_block, axis=(0, 1))
    pointwise_part = jnp.einsum(
        "krf,krd->fd", middle_act, grad_mixed, preferred_element_type=jnp.float32
    )
    grad_middle = jnp.einsum(
        "krd,fd->krf", grad_mixed, pointwise_low, preferred_element_type=jnp.float32
    )
    grad_middle_pre = middle_back(grad_middle * valid_mask)[0]
    middle_gain_part = jnp.sum(grad_middle_pre * middle_norm, axis=(0, 1))
    middle_shift_part = jnp.sum(grad_middle_pre, axis=(0, 1))
    (
        middle_gain_gradient,
        middle_shift_gradient,
        pointwise_kernel_gradient,
        pointwise_bias_gradient,
    ) = lax.psum((middle_gain_part, middle_shift_part, pointwise_part, bias_part), ("grp", "seq"))
    dilated_gradient = (
        middle_gain
        * middle_scale
        * (
            grad_middle_pre
            - (middle_shift_gradient + middle_norm * middle_gain_gradient) / row_count
        )
        * valid_mask
    )
    dilated_gradient = dilated_gradient.astype(jnp.bfloat16)
    border_gradient = from_partner(
        dilated_gradient[:, HALF_WINDOW_ROWS - DILATION_STEP : HALF_WINDOW_ROWS + DILATION_STEP],
        "seq",
        0,
    )
    grad_wide = extended(dilated_gradient, border_gradient)
    grad_halves = dilated_gradient.reshape(2 * position_count, HALF_WINDOW_ROWS, -1)
    kernel_pieces = []
    grad_entry = jnp.zeros((2 * position_count, HALF_WINDOW_ROWS, channel_width), jnp.float32)
    for kernel_tap_index in range(3):
        displaced_rows = entry_widened[
            :,
            kernel_tap_index * DILATION_STEP : kernel_tap_index * DILATION_STEP + HALF_WINDOW_ROWS,
        ]
        kernel_pieces.append(
            jnp.einsum(
                "hrc,hrf->cf", displaced_rows, grad_halves, preferred_element_type=jnp.float32
            )
        )
        backward_offset = (2 - kernel_tap_index) * DILATION_STEP
        grad_shifted = grad_wide[:, backward_offset : backward_offset + HALF_WINDOW_ROWS]
        grad_entry = grad_entry + jnp.einsum(
            "hrf,cf->hrc",
            grad_shifted,
            kernel_low[kernel_tap_index],
            preferred_element_type=jnp.float32,
        )
    kernel_part = jnp.stack(kernel_pieces)
    grad_entry = grad_entry.reshape(position_count, WINDOW_SPAN, channel_width)
    grad_entry_pre = entry_back(grad_entry * valid_mask)[0]
    entry_gain_part = jnp.sum(grad_entry_pre * entry_norm, axis=(0, 1))
    entry_shift_part = jnp.sum(grad_entry_pre, axis=(0, 1))
    entry_gain_gradient, entry_shift_gradient, dilated_kernel_gradient = lax.psum(
        (entry_gain_part, entry_shift_part, kernel_part), ("grp", "seq")
    )
    grad_pooled = (
        entry_gain
        * entry_scale
        * (grad_entry_pre - (entry_shift_gradient + entry_norm * entry_gain_gradient) / row_count)
        * valid_mask
        + grad_block
    )
    returned = lax.all_to_all(
        grad_pooled.astype(jnp.bfloat16), "seq", split_axis=1, concat_axis=0, tiled=True
    )
    inverse = (
        jnp.zeros((group_windows,), jnp.int32)
        .at[picked]
        .set(jnp.arange(group_windows, dtype=jnp.int32))
    )
    grad_source = jnp.take(returned, inverse, axis=0).astype(jnp.float32) * source_valid
    zero_part = jnp.zeros_like(grad_source)
    signal_gradient = jnp.stack(
        [
            jnp.where(take_first, grad_source, zero_part),
            jnp.where(take_first, zero_part, grad_source),
        ],
        axis=2,
    ).reshape(group_windows, segment, channel_width)
    return (
        activations,
        signal_gradient,
        entry_gain_gradient,
        entry_shift_gradient,
        dilated_kernel_gradient,
        middle_gain_gradient,
        middle_shift_gradient,
        pointwise_kernel_gradient,
        pointwise_bias_gradient,
    )


def solution(mesh):
    return jax.shard_map(
        per_device,
        mesh=mesh,
        in_specs=(
            P("grp", "seq", None),
            P(),
            P(),
            P(),
            P(),
            P(),
            P(),
            P(),
            P(),
            P("grp", None),
            P(("grp", "seq"), None),
        ),
        out_specs=(
            P(("grp", "seq"), None),
            P("grp", "seq", None),
            P(),
            P(),
            P(),
            P(),
            P(),
            P(),
            P(),
        ),
        check_vma=False,
    )
```

profile of v0, /device:TPU:0, one launch (start us, length us, event | category | flops | bytes accessed | tf_op | source)
XLA Modules:
  0.0 660.3 jit_solution(9878125855591612174)
XLA Ops:
  8.7 16.6 %copy.79 = f32[16,256,768]{2,0,1:T(8,128)} copy(f32[16,256,768]{2,1,0:T(8,128)} %param.15) | data formatting | bytes 25165824 | tf_op args[0]
  25.4 10.5 %fusion.86 = (f32[16,128,1,768]{3,0,2,1:T(8,128)}, f32[16,128,1,768]{3,0,2,1:T(8,128)}) fusion(f32[16,128,2,768]{3,0,2,1:T(8,128)} %bitcast.168), kind=kLoop, calls=%fused_computation.166 | loop fusion | bytes 25165824 | tf_op jit(solution)/shard_map/slice | solution.py:71
  36.1 11.7 %multiply_convert_fusion.1 = (bf16[16,128,768]{2,1,0:T(8,128)(2,1)}, pred[16,128,768]{2,1,0:T(8,128)(4,1)}) fusion(f32[16,128,1,768]{3,0,2,1:T(8,128)} %get-tuple-element.66, f32[16,128,1,768]{3,0,2,1:T(8,128)} %get-tuple-element.65, f32[16,128]{1,0:T(8,128)S(1)} %compare_convert_fusion.2), kind=kLoop, calls=%fused_computation.48 | loop fusion | flops 6291456 | bytes 17309696 | tf_op jit(solution)/shard_map/convert_element_type | solution.py:78
  52.4 7.4 %all-to-all-start = ((bf16[16,128,768]{2,1,0:T(8,128)(2,1)}), bf16[16,128,768]{2,1,0:T(8,128)(2,1)S(1)}, u32[]{:S(2)}, u32[]{:S(2)}) async-start(bf16[16,128,768]{2,1,0:T(8,128)(2,1)} %broadcast_select_fusion.1), calls=%async_computation | async-start | bytes 6291456 | tf_op jit(solution)/shard_map/all_to_all | solution.py:89
  61.7 3.7 convert_element_type.105
  66.3 5.2 multiply_convert_fusion.2
  71.5 3.5 fusion.38
  75.1 55.5 %all-to-all-done = bf16[16,128,768]{2,1,0:T(8,128)(2,1)S(1)} async-done(((bf16[16,128,768]{2,1,0:T(8,128)(2,1)}), bf16[16,128,768]{2,1,0:T(8,128)(2,1)S(1)}, u32[]{:S(2)}, u32[]{:S(2)}) %all-to-all-start) | async-done | bytes 3145760 | tf_op jit(solution)/shard_map/all_to_all | solution.py:89
  131.3 37.8 %psum.77 = f32[768]{0:T(1024)S(1)} all-reduce(f32[768]{0:T(1024)S(1)} %multiply_reduce_fusion.2), channel_id=1, replica_groups=mesh['grp'=4,'seq'=8] {'grp','seq'}, use_global_device_ids=true, to_apply=%region_1.4 | all-reduce | flops 768 | bytes 6144 | tf_op jit(solution)/shard_map/psum | solution.py:27
  170.8 41.7 %psum.78 = f32[768]{0:T(1024)S(1)} all-reduce(f32[768]{0:T(1024)S(1)} %multiply_reduce_fusion.1), channel_id=1, replica_groups=mesh['grp'=4,'seq'=8] {'grp','seq'}, use_global_device_ids=true, to_apply=%region_4.7 | all-reduce | flops 768 | bytes 6144 | tf_op jit(solution)/shard_map/psum | solution.py:29
  214.6 3.4 multiply_convert_fusion
  220.6 4.9 collective-permute-done
  234.9 38.2 %psum.79 = f32[384]{0:T(512)S(1)} all-reduce(f32[384]{0:T(512)S(1)} %get-tuple-element.86), channel_id=1, replica_groups=mesh['grp'=4,'seq'=8] {'grp','seq'}, use_global_device_ids=true, to_apply=%region_6.9 | all-reduce | flops 384 | bytes 3072 | tf_op jit(solution)/shard_map/psum | solution.py:27
  274.2 41.7 %psum.80 = f32[384]{0:T(512)S(1)} all-reduce(f32[384]{0:T(512)S(1)} %multiply_reduce_fusion.5), channel_id=1, replica_groups=mesh['grp'=4,'seq'=8] {'grp','seq'}, use_global_device_ids=true, to_apply=%region_8.11 | all-reduce | flops 384 | bytes 3072 | tf_op jit(solution)/shard_map/psum | solution.py:29
  316.6 6.1 fusion.81
  322.7 38.7 %all-reduce.1 = (f32[384]{0:T(512)S(1)}, f32[384]{0:T(512)S(1)}) all-reduce(f32[384]{0:T(512)S(1)} %get-tuple-element.50, f32[384]{0:T(512)S(1)} %get-tuple-element.49), channel_id=1, replica_groups=mesh['grp'=4,'seq'=8] {'grp','seq'}, use_global_device_ids=true, to_apply=%region_12.15 | all-reduce | flops 768 | bytes 6144 | tf_op jit(solution)/shard_map/psum | solution.py:156
  361.4 3.0 multiply_convert_fusion.5
  367.0 2.7 collective-permute-done.1
  375.3 8.2 %fusion.80 = (f32[768]{0:T(1024)S(1)}, f32[768]{0:T(1024)S(1)}, f32[4,512,768]{2,1,0:T(8,128)}) fusion(f32[768]{0:T(1024)S(1)} %get-tuple-element.59, f32[4,512,768]{2,1,0:T(8,128)S(1)} %bitcast.163, f32[768]{0:T(1024)S(1)} %broadcast_divide_fusion, f32[768]{0:T(1024)S(1)} %copy-done.15, f32[768]{0:T(1024)S(1)} %copy-done.13, f32[4,512]{1,0:T(4,128)S(1)} %fusion.74, ...), kind=kOutput, calls=%fused_computation.162 | convolution fusion | flops 1253571072 | bytes 27359232 | tf_op jit(solution)/shard_map/hrf,cf->hrc/dot_general | solution.py:188
  383.5 41.3 %all-reduce = (f32[768]{0:T(1024)S(1)}, f32[768]{0:T(1024)S(1)}, f32[768]{0:T(1024)}) all-reduce(f32[768]{0:T(1024)S(1)} %get-tuple-element.48, f32[768]{0:T(1024)S(1)} %get-tuple-element.47, f32[768]{0:T(1024)S(1)} %get-tuple-element.68), channel_id=1, replica_groups=mesh['grp'=4,'seq'=8] {'grp','seq'}, use_global_device_ids=true, to_apply=%region_16.19 | all-reduce | flops 2304 | bytes 18432 | tf_op jit(solution)/shard_map/psum | solution.py:199
  424.8 11.1 %fusion.10 = bf16[2,1024,768]{2,1,0:T(8,128)(2,1)S(1)} fusion(f32[2,1024,768]{2,1,0:T(8,128)} %bitcast.164, f32[2,8,128,768]{3,2,1,0:T(8,128)} %copy-done.1, f32[]{:T(128)} %convert_reduce_fusion, f32[768]{0:T(1024)S(1)} %get-tuple-element.95, f32[768]{0:T(1024)S(1)} %get-tuple-element.96, f32[768]{0:T(1024)S(1)} %get-tuple-element.58, ...), kind=kLoop, calls=%fused_computation.21 | loop fusion | flops 51904512 | bytes 22049796 | tf_op jit(solution)/shard_map/convert_element_type | solution.py:210
  435.9 5.0 copy.86
  440.9 5.2 all-to-all-start.1
  446.2 4.3 fusion.60
  462.3 7.3 %fusion.19 = f32[2,1024,768]{2,1,0:T(8,128)} fusion(f32[2,8,128,768]{3,2,1,0:T(8,128)} %copy-done.1, f32[768]{0:T(1024)S(1)} %copy-done.17, f32[2,1024]{1,0:T(2,128)S(1)} %compare_convert_fusion.1, bf16[2,1024,384]{2,1,0:T(8,128)(2,1)S(1)} %copy-done.5, f32[384,768]{1,0:T(8,128)S(1)} %copy-done.7), kind=kOutput, calls=%fused_computation.36 | convolution fusion | flops 1212973056 | bytes 15346688 | tf_op jit(solution)/shard_map/krf,fd->krd/dot_general | solution.py:135
  469.6 68.6 %all-to-all-done.1 = bf16[2,1024,768]{2,0,1:T(2,128)(2,1)} async-done(((bf16[2,1024,768]{2,0,1:T(2,128)(2,1)}), bf16[2,1024,768]{2,0,1:T(2,128)(2,1)}, u32[]{:S(2)}, u32[]{:S(2)}) %all-to-all-start.1) | async-done | bytes 3145760 | tf_op jit(solution)/shard_map/all_to_all | solution.py:209
  543.1 5.3 select_bitcast_fusion.1
  548.4 9.2 %pad_maximum_fusion = f32[16,128,2,768]{3,1,0,2:T(8,128)} fusion(f32[16,128,1,768]{3,1,0,2:T(8,128)} %get-tuple-element.70, f32[16,128,1,768]{3,1,0,2:T(8,128)S(1)} %get-tuple-element.69), kind=kLoop, calls=%fused_computation.6 | loop fusion | flops 3145728 | bytes 25165824 | tf_op jit(solution)/shard_map/stack | solution.py:219
  557.6 16.5 %copy.89 = f32[16,128,2,768]{3,0,2,1:T(8,128)} copy(f32[16,128,2,768]{3,1,0,2:T(8,128)} %pad_maximum_fusion) | data formatting | bytes 25165824 | tf_op jit(solution)/shard_map/stack | solution.py:219
  574.0 16.9 %copy.94 = f32[16,256,768]{2,1,0:T(8,128)} copy(f32[16,256,768]{2,0,1:T(8,128)} %bitcast.169) | data formatting | bytes 25165824
  590.9 57.0 %all-reduce.5.cloned.1.call-done = (f32[3,768,384]{2,1,0:T(8,128)}, f32[384,768]{1,0:T(8,128)}) async-done(((f32[3,768,384]{2,1,0:T(8,128)}, f32[384,768]{1,0:T(8,128)}), (f32[3,768,384]{2,1,0:T(8,128)}, f32[384,768]{1,0:T(8,128)})) %all-reduce.5.cloned.1.call-update) | async-done | bytes 4718608 | tf_op jit(solution)/shard_map/psum | solution.py:199
  647.9 4.1 copy.127
  (144 shorter events, 53.0 us)
Async XLA Ops:
  25.4 10.5 %copy-start.22 = (s32[64]{0:T(128)S(1)}, s32[64]{0:T(128)}, u32[]{:S(2)}) copy-start(s32[64]{0:T(128)} %param.23) | copy-start | bytes 772
  52.4 7.5 %copy-start = (s32[1,16]{1,0:T(1,128)S(1)}, s32[1,16]{1,0:T(1,128)}, u32[]{:S(2)}) copy-start(s32[1,16]{1,0:T(1,128)} %param.24) | copy-start | bytes 196
  52.4 78.1 %all-to-all-start = ((bf16[16,128,768]{2,1,0:T(8,128)(2,1)}), bf16[16,128,768]{2,1,0:T(8,128)(2,1)S(1)}, u32[]{:S(2)}, u32[]{:S(2)}) async-start(bf16[16,128,768]{2,1,0:T(8,128)(2,1)} %broadcast_select_fusion.1), calls=%async_computation | async-start | bytes 6291456 | tf_op jit(solution)/shard_map/all_to_all | solution.py:89
  61.7 9.9 %slice-start.2 = ((s8[6291456]{0:T(1024)(128)(4,1)}), s8[4194304]{0:T(1024)(128)(4,1)S(1)}, s32[]{:S(2)}) async-start(s8[6291456]{0:T(1024)(128)(4,1)} %bitcast.165), calls=%async_computation.5 | async-start | bytes 8388608
  66.3 5.2 slice-start.3
  66.3 5.2 copy-start.6
  213.2 0.7 copy-start.13
  213.2 1.3 copy-start.15
  213.9 4.1 copy-start.1
  218.1 7.4 %collective-permute-start = (bf16[2,76,768]{2,1,0:T(8,128)(2,1)S(1)}, bf16[2,76,768]{2,1,0:T(8,128)(2,1)S(1)}, u32[]{:S(2)}, u32[]{:S(2)}) collective-permute-start(bf16[2,76,768]{2,1,0:T(8,128)(2,1)S(1)} %slice.103), channel_id=1, source_target_pairs={{0,1},{1,0},{2,3},{3,2},{4,5},{5,4},{6,7},{7,6},{8,9},{9,8},{10,11... | collective-permute-start | bytes 700424 | tf_op jit(solution)/shard_map/ppermute | solution.py:19
  227.0 2.1 copy-start.10
  227.3 5.6 copy-start.8
  234.9 81.1 %copy-start.14 = (f32[384]{0:T(512)S(1)}, f32[384]{0:T(512)}, u32[]{:S(2)}) copy-start(f32[384]{0:T(512)} %param.19) | copy-start | bytes 4612
  234.9 81.7 %copy-start.16 = (f32[384]{0:T(512)S(1)}, f32[384]{0:T(512)}, u32[]{:S(2)}) copy-start(f32[384]{0:T(512)} %param.20) | copy-start | bytes 4612
  361.4 3.1 copy-start.20
  361.4 3.1 copy-start.21
  364.4 2.4 copy-start.3
  364.5 5.2 collective-permute-start.1
  370.2 1.5 copy-start.11
  370.4 4.9 slice-start
  371.6 3.7 slice-start.1
  424.8 11.1 %copy-start.18 = (f32[768]{0:T(1024)}, f32[768]{0:T(1024)S(1)}, u32[]{:S(2)}) copy-start(f32[768]{0:T(1024)S(1)} %get-tuple-element.95) | copy-start | bytes 9220
  424.8 11.1 %copy-start.19 = (f32[768]{0:T(1024)}, f32[768]{0:T(1024)S(1)}, u32[]{:S(2)}) copy-start(f32[768]{0:T(1024)S(1)} %get-tuple-element.96) | copy-start | bytes 9220
  440.9 97.2 %all-to-all-start.1 = ((bf16[2,1024,768]{2,0,1:T(2,128)(2,1)}), bf16[2,1024,768]{2,0,1:T(2,128)(2,1)}, u32[]{:S(2)}, u32[]{:S(2)}) async-start(bf16[2,1024,768]{2,0,1:T(2,128)(2,1)} %copy.86), calls=%async_computation.1 | async-start | bytes 6291456 | tf_op jit(solution)/shard_map/all_to_all | solution.py:209
  446.1 201.8 %all-reduce.5.cloned.1.call-start = ((), (), s32[]{:S(2)}) async-start(), calls=%async_computation.2 | async-start | bytes 9437184 | tf_op jit(solution)/shard_map/psum | solution.py:199
  446.2 4.3 copy-start.4
  446.2 4.3 copy-start.9
  456.2 1.9 copy-start.2
  460.5 1.4 copy-start.5
  460.5 1.7 copy-start.7
  460.5 1.7 copy-start.17
  647.9 4.1 copy-start.12
Sparse Core Ops, SparseCore 0:
  460.7 187.1 all-reduce.4
where the time goes:
time: 668 us; the launch traced here: 660 us
  blocking collectives  239 us (36%)
  waiting for transfers between devices  189 us (28%)
  local copies, waits for them, and re-layouts  88.1 us (13%)
  other arithmetic  73 us (11%)
  matrix products  38.7 us (6%)
  starting transfers between devices  17.3 us (3%)
  between operations  15.1 us (2%)
    psum x2, blocking collectives, moments(): lax.psum(jnp.sum(deviation * deviation, axis=(0, 1)), ('grp', 'seq'))  83.4 us
    psum x2, blocking collectives, moments(): lax.psum(jnp.sum(values * valid_mask, axis=(0, 1)), ('grp', 'seq'))  76 us
    all_to_all x1, waiting for transfers between devices, per_device(): lax.all_to_all(grad_pooled.astype(jnp.bfloat16), 'seq', split_axis=1, con...  68.6 us
    psum x1, waiting for transfers between devices, per_device(): lax.psum((entry_gain_part, entry_shift_part, kernel_part), ('grp', 'seq'))  57 us
    all_to_all x1, waiting for transfers between devices, per_device(): lax.all_to_all(outgoing, 'seq', split_axis=0, concat_axis=1, tiled=True)  55.5 us
    unnamed x61, local copies, waits for them, and re-layouts  43.3 us
    psum x1, blocking collectives, per_device(): lax.psum((entry_gain_part, entry_shift_part, kernel_part), ('grp', 'seq'))  41.3 us
    psum x1, blocking collectives, per_device(): lax.psum((middle_gain_part, middle_shift_part, pointwise_part, bias_part)...  38.7 us
  transfers between devices with their start and end apart: 5, of which 5 were waited for; matrix products, arithmetic and copies ran while one was open for 14% of the time, Pallas kernels for 0%

commit v1 on v0

--- a/solution.py
+++ b/solution.py
@@ -26,7 +26,10 @@
 def moments(values, valid_mask, row_count):
     centre = lax.psum(jnp.sum(values * valid_mask, axis=(0, 1)), ("grp", "seq")) / row_count
     deviation = (values - centre) * valid_mask
-    spread = lax.psum(jnp.sum(deviation * deviation, axis=(0, 1)), ("grp", "seq")) / row_count
+    spread = (
+        jnp.sum(lax.all_gather(jnp.sum(deviation * deviation, axis=(0, 1)), ("grp", "seq")), axis=0)
+        / row_count
+    )
     return (centre, lax.rsqrt(spread + EPSILON))
 
 

time: 668 us -> 717 us (1.073)
  blocking collectives: 239 us -> 286 us
    all_gather x0 -> x2, blocking collectives: none -> 133 us  [moments(): lax.all_gather(jnp.sum(deviation * deviation, axis=(0, 1)), ('grp', 'seq'))]
    psum x2 -> x0, blocking collectives: 83.4 us -> none  [moments(): lax.psum(jnp.sum(deviation * deviation, axis=(0, 1)), ('grp', 'seq'))]
  transfers between devices with their start and end apart: 5 -> 5, of which waited for: 5 -> 5; matrix products, arithmetic and copies ran while one was open for 14% -> 13% of each run, Pallas kernels for 0% -> 0%
where the time goes in v1:
time: 717 us; the launch traced here: 710 us
  blocking collectives  286 us (40%)
  waiting for transfers between devices  189 us (26%)
  local copies, waits for them, and re-layouts  90.6 us (13%)
  other arithmetic  74.5 us (10%)
  matrix products  38.7 us (5%)
  between operations  15.1 us (2%)
  starting transfers between devices  14.8 us (2%)
    all_gather x2, blocking collectives, moments(): lax.all_gather(jnp.sum(deviation * deviation, axis=(0, 1)), ('grp', 'seq'))  133 us
    psum x2, blocking collectives, moments(): lax.psum(jnp.sum(values * valid_mask, axis=(0, 1)), ('grp', 'seq'))  74.7 us
    all_to_all x1, waiting for transfers between devices, per_device(): lax.all_to_all(grad_pooled.astype(jnp.bfloat16), 'seq', split_axis=1, con...  68.8 us
    psum x1, waiting for transfers between devices, per_device(): lax.psum((entry_gain_part, entry_shift_part, kernel_part), ('grp', 'seq'))  56.5 us
    all_to_all x1, waiting for transfers between devices, per_device(): lax.all_to_all(outgoing, 'seq', split_axis=0, concat_axis=1, tiled=True)  55.5 us
    unnamed x61, local copies, waits for them, and re-layouts  43 us
    psum x1, blocking collectives, per_device(): lax.psum((entry_gain_part, entry_shift_part, kernel_part), ('grp', 'seq'))  41.8 us
    psum x1, blocking collectives, per_device(): lax.psum((middle_gain_part, middle_shift_part, pointwise_part, bias_part)...  37.3 us
  transfers between devices with their start and end apart: 5, of which 5 were waited for; matrix products, arithmetic and copies ran while one was open for 13% of the time, Pallas kernels for 0%

profile of v1, /device:TPU:0, one launch (start us, length us, event | category | flops | bytes accessed | tf_op | source)
XLA Modules:
  0.0 709.5 jit_solution(8648982790237815369)
XLA Ops:
  8.7 16.6 %copy.79 = f32[16,256,768]{2,0,1:T(8,128)} copy(f32[16,256,768]{2,1,0:T(8,128)} %param.15) | data formatting | bytes 25165824 | tf_op args[0]
  25.4 10.5 %fusion.86 = (f32[16,128,1,768]{3,0,2,1:T(8,128)}, f32[16,128,1,768]{3,0,2,1:T(8,128)}) fusion(f32[16,128,2,768]{3,0,2,1:T(8,128)} %bitcast.168), kind=kLoop, calls=%fused_computation.166 | loop fusion | bytes 25165824 | tf_op jit(solution)/shard_map/slice | solution.py:74
  36.1 11.3 %multiply_convert_fusion.1 = (bf16[16,128,768]{2,1,0:T(8,128)(2,1)}, pred[16,128,768]{2,1,0:T(8,128)(4,1)}) fusion(f32[16,128,1,768]{3,0,2,1:T(8,128)} %get-tuple-element.66, f32[16,128,1,768]{3,0,2,1:T(8,128)} %get-tuple-element.65, f32[16,128]{1,0:T(8,128)S(1)} %compare_convert_fusion.2), kind=kLoop, calls=%fused_computation.48 | loop fusion | flops 6291456 | bytes 17309696 | tf_op jit(solution)/shard_map/convert_element_type | solution.py:81
  52.1 7.4 %all-to-all-start = ((bf16[16,128,768]{2,1,0:T(8,128)(2,1)}), bf16[16,128,768]{2,1,0:T(8,128)(2,1)S(1)}, u32[]{:S(2)}, u32[]{:S(2)}) async-start(bf16[16,128,768]{2,1,0:T(8,128)(2,1)} %broadcast_select_fusion.1), calls=%async_computation | async-start | bytes 6291456 | tf_op jit(solution)/shard_map/all_to_all | solution.py:92
  61.3 3.6 convert_element_type.105
  66.0 5.2 multiply_convert_fusion.2
  71.2 3.5 fusion.38
  74.7 55.5 %all-to-all-done = bf16[16,128,768]{2,1,0:T(8,128)(2,1)S(1)} async-done(((bf16[16,128,768]{2,1,0:T(8,128)(2,1)}), bf16[16,128,768]{2,1,0:T(8,128)(2,1)S(1)}, u32[]{:S(2)}, u32[]{:S(2)}) %all-to-all-start) | async-done | bytes 3145760 | tf_op jit(solution)/shard_map/all_to_all | solution.py:92
  130.9 37.8 %psum.63 = f32[768]{0:T(1024)S(1)} all-reduce(f32[768]{0:T(1024)S(1)} %multiply_reduce_fusion.2), channel_id=1, replica_groups=mesh['grp'=4,'seq'=8] {'grp','seq'}, use_global_device_ids=true, to_apply=%region_1.4 | all-reduce | flops 768 | bytes 6144 | tf_op jit(solution)/shard_map/psum | solution.py:27
  170.5 66.4 %all-gather.2 = f32[32,1,768]{2,1,0:T(1,128)S(1)} all-gather(f32[1,1,768]{2,1,0:T(1,128)S(1)} %reshape.342), channel_id=2, replica_groups=mesh['grp'=4,'seq'=8] {'grp','seq'}, dimensions={0}, use_global_device_ids=true | all-gather | bytes 101376 | tf_op jit(solution)/shard_map/all_gather | solution.py:30
  237.6 3.3 copy.82
  241.7 5.1 multiply_convert_fusion
  247.2 6.0 collective-permute-done
  262.5 36.9 %psum.64 = f32[384]{0:T(512)S(1)} all-reduce(f32[384]{0:T(512)S(1)} %get-tuple-element.86), channel_id=1, replica_groups=mesh['grp'=4,'seq'=8] {'grp','seq'}, use_global_device_ids=true, to_apply=%region_6.9 | all-reduce | flops 384 | bytes 3072 | tf_op jit(solution)/shard_map/psum | solution.py:27
  300.6 66.1 %all-gather.3 = f32[32,1,384]{2,1,0:T(1,128)S(1)} all-gather(f32[1,1,384]{2,1,0:T(1,128)S(1)} %reshape.344), channel_id=3, replica_groups=mesh['grp'=4,'seq'=8] {'grp','seq'}, dimensions={0}, use_global_device_ids=true | all-gather | bytes 50688 | tf_op jit(solution)/shard_map/all_gather | solution.py:30
  367.5 6.1 fusion.81
  373.5 37.3 %all-reduce.1 = (f32[384]{0:T(512)S(1)}, f32[384]{0:T(512)S(1)}) all-reduce(f32[384]{0:T(512)S(1)} %get-tuple-element.50, f32[384]{0:T(512)S(1)} %get-tuple-element.49), channel_id=1, replica_groups=mesh['grp'=4,'seq'=8] {'grp','seq'}, use_global_device_ids=true, to_apply=%region_12.15 | all-reduce | flops 768 | bytes 6144 | tf_op jit(solution)/shard_map/psum | solution.py:159
  410.8 3.0 multiply_convert_fusion.5
  424.8 8.1 %fusion.80 = (f32[768]{0:T(1024)S(1)}, f32[768]{0:T(1024)S(1)}, f32[4,512,768]{2,1,0:T(8,128)}) fusion(f32[768]{0:T(1024)S(1)} %get-tuple-element.59, f32[4,512,768]{2,1,0:T(8,128)S(1)} %bitcast.163, f32[768]{0:T(1024)S(1)} %broadcast_divide_fusion, f32[768]{0:T(1024)S(1)} %copy-done.14, f32[768]{0:T(1024)S(1)} %copy-done.12, f32[4,512]{1,0:T(4,128)S(1)} %fusion.74, ...), kind=kOutput, calls=%fused_computation.162 | convolution fusion | flops 1253571072 | bytes 27359232 | tf_op jit(solution)/shard_map/hrf,cf->hrc/dot_general | solution.py:191
  432.9 41.8 %all-reduce = (f32[768]{0:T(1024)S(1)}, f32[768]{0:T(1024)S(1)}, f32[768]{0:T(1024)}) all-reduce(f32[768]{0:T(1024)S(1)} %get-tuple-element.48, f32[768]{0:T(1024)S(1)} %get-tuple-element.47, f32[768]{0:T(1024)S(1)} %get-tuple-element.68), channel_id=1, replica_groups=mesh['grp'=4,'seq'=8] {'grp','seq'}, use_global_device_ids=true, to_apply=%region_16.19 | all-reduce | flops 2304 | bytes 18432 | tf_op jit(solution)/shard_map/psum | solution.py:202
  474.7 11.1 %fusion.10 = bf16[2,1024,768]{2,1,0:T(8,128)(2,1)S(1)} fusion(f32[2,1024,768]{2,1,0:T(8,128)} %bitcast.164, f32[2,8,128,768]{3,2,1,0:T(8,128)} %copy.82, f32[]{:T(128)} %convert_reduce_fusion, f32[768]{0:T(1024)S(1)} %get-tuple-element.95, f32[768]{0:T(1024)S(1)} %get-tuple-element.96, f32[768]{0:T(1024)S(1)} %get-tuple-element.58, f32[768]{0:T(1024)S(1)} %copy-done.14, ...), kind=kLoop, calls=%fused_computation.21 | loop fusion | flops 51904512 | bytes 22049796 | tf_op jit(solution)/shard_map/convert_element_type | solution.py:213
  485.8 5.0 copy.86
  490.8 5.0 all-to-all-start.1
  495.8 4.3 fusion.60
  511.9 7.3 %fusion.19 = f32[2,1024,768]{2,1,0:T(8,128)} fusion(f32[2,8,128,768]{3,2,1,0:T(8,128)} %copy.82, f32[768]{0:T(1024)S(1)} %copy-done.16, f32[2,1024]{1,0:T(2,128)S(1)} %compare_convert_fusion.1, bf16[2,1024,384]{2,1,0:T(8,128)(2,1)S(1)} %copy-done.4, f32[384,768]{1,0:T(8,128)S(1)} %copy-done.6), kind=kOutput, calls=%fused_computation.36 | convolution fusion | flops 1212973056 | bytes 15346688 | tf_op jit(solution)/shard_map/krf,fd->krd/dot_general | solution.py:138
  519.2 68.8 %all-to-all-done.1 = bf16[2,1024,768]{2,0,1:T(2,128)(2,1)} async-done(((bf16[2,1024,768]{2,0,1:T(2,128)(2,1)}), bf16[2,1024,768]{2,0,1:T(2,128)(2,1)}, u32[]{:S(2)}, u32[]{:S(2)}) %all-to-all-start.1) | async-done | bytes 3145760 | tf_op jit(solution)/shard_map/all_to_all | solution.py:212
  593.0 5.1 select_bitcast_fusion.1
  598.1 9.1 %pad_maximum_fusion = f32[16,128,2,768]{3,1,0,2:T(8,128)} fusion(f32[16,128,1,768]{3,1,0,2:T(8,128)} %get-tuple-element.70, f32[16,128,1,768]{3,1,0,2:T(8,128)S(1)} %get-tuple-element.69), kind=kLoop, calls=%fused_computation.6 | loop fusion | flops 3145728 | bytes 25165824 | tf_op jit(solution)/shard_map/stack | solution.py:222
  607.2 16.5 %copy.89 = f32[16,128,2,768]{3,0,2,1:T(8,128)} copy(f32[16,128,2,768]{3,1,0,2:T(8,128)} %pad_maximum_fusion) | data formatting | bytes 25165824 | tf_op jit(solution)/shard_map/stack | solution.py:222
  623.8 16.9 %copy.94 = f32[16,256,768]{2,1,0:T(8,128)} copy(f32[16,256,768]{2,0,1:T(8,128)} %bitcast.169) | data formatting | bytes 25165824
  640.6 56.5 %all-reduce.5.cloned.1.call-done = (f32[3,768,384]{2,1,0:T(8,128)}, f32[384,768]{1,0:T(8,128)}) async-done(((f32[3,768,384]{2,1,0:T(8,128)}, f32[384,768]{1,0:T(8,128)}), (f32[3,768,384]{2,1,0:T(8,128)}, f32[384,768]{1,0:T(8,128)})) %all-reduce.5.cloned.1.call-update) | async-done | bytes 4718608 | tf_op jit(solution)/shard_map/psum | solution.py:202
  697.1 4.1 copy.127
  (146 shorter events, 52.9 us)
Async XLA Ops:
  25.4 10.6 %copy-start.21 = (s32[64]{0:T(128)S(1)}, s32[64]{0:T(128)}, u32[]{:S(2)}) copy-start(s32[64]{0:T(128)} %param.23) | copy-start | bytes 772
  52.1 7.5 %copy-start = (s32[1,16]{1,0:T(1,128)S(1)}, s32[1,16]{1,0:T(1,128)}, u32[]{:S(2)}) copy-start(s32[1,16]{1,0:T(1,128)} %param.24) | copy-start | bytes 196
  52.1 78.1 %all-to-all-start = ((bf16[16,128,768]{2,1,0:T(8,128)(2,1)}), bf16[16,128,768]{2,1,0:T(8,128)(2,1)S(1)}, u32[]{:S(2)}, u32[]{:S(2)}) async-start(bf16[16,128,768]{2,1,0:T(8,128)(2,1)} %broadcast_select_fusion.1), calls=%async_computation | async-start | bytes 6291456 | tf_op jit(solution)/shard_map/all_to_all | solution.py:92
  61.3 9.8 %slice-start.2 = ((s8[6291456]{0:T(1024)(128)(4,1)}), s8[4194304]{0:T(1024)(128)(4,1)S(1)}, s32[]{:S(2)}) async-start(s8[6291456]{0:T(1024)(128)(4,1)} %bitcast.165), calls=%async_computation.5 | async-start | bytes 8388608
  66.0 5.2 slice-start.3
  66.0 5.2 copy-start.5
  237.6 3.4 copy-start.12
  237.6 4.1 copy-start.14
  246.9 6.3 collective-permute-start
  254.7 2.1 copy-start.9
  254.9 5.5 copy-start.7
  262.5 104.3 %copy-start.13 = (f32[384]{0:T(512)S(1)}, f32[384]{0:T(512)}, u32[]{:S(2)}) copy-start(f32[384]{0:T(512)} %param.19) | copy-start | bytes 4612
  262.5 104.9 %copy-start.15 = (f32[384]{0:T(512)S(1)}, f32[384]{0:T(512)}, u32[]{:S(2)}) copy-start(f32[384]{0:T(512)} %param.20) | copy-start | bytes 4612
  410.8 3.1 copy-start.19
  410.8 3.1 copy-start.20
  413.9 2.4 copy-start.2
  413.9 5.2 collective-permute-start.1
  419.6 1.5 copy-start.10
  419.8 4.9 slice-start
  421.1 3.7 slice-start.1
  474.7 11.1 %copy-start.17 = (f32[768]{0:T(1024)}, f32[768]{0:T(1024)S(1)}, u32[]{:S(2)}) copy-start(f32[768]{0:T(1024)S(1)} %get-tuple-element.95) | copy-start | bytes 9220
  474.7 11.1 %copy-start.18 = (f32[768]{0:T(1024)}, f32[768]{0:T(1024)S(1)}, u32[]{:S(2)}) copy-start(f32[768]{0:T(1024)S(1)} %get-tuple-element.96) | copy-start | bytes 9220
  490.8 97.2 %all-to-all-start.1 = ((bf16[2,1024,768]{2,0,1:T(2,128)(2,1)}), bf16[2,1024,768]{2,0,1:T(2,128)(2,1)}, u32[]{:S(2)}, u32[]{:S(2)}) async-start(bf16[2,1024,768]{2,0,1:T(2,128)(2,1)} %copy.86), calls=%async_computation.1 | async-start | bytes 6291456 | tf_op jit(solution)/shard_map/all_to_all | solution.py:212
  495.8 201.3 %all-reduce.5.cloned.1.call-start = ((), (), s32[]{:S(2)}) async-start(), calls=%async_computation.2 | async-start | bytes 9437184 | tf_op jit(solution)/shard_map/psum | solution.py:202
  495.8 4.3 copy-start.3
  495.8 4.3 copy-start.8
  505.9 1.9 copy-start.1
  510.2 1.4 copy-start.4
  510.2 1.7 copy-start.6
  510.2 1.7 copy-start.16
  697.1 4.1 copy-start.11
Sparse Core Ops, SparseCore 0:
  510.3 186.7 all-reduce.4
